TPU v7x, 32 devices: a whole 2x2x4 slice. The times are simulated.
32 devices in a mesh: slab: 4 (over y, x), cross: 8 (over z, core).
Axes of the slice: x: 2, y: 2, z: 4, core: 2. Of those that a mesh axis runs over, the one named last changes fastest.
Arguments:
- rhs: bfloat16 [4, 8, 32, 128, 128], P('slab', 'cross'), may hold values from -6 to 6
- m_blocks: bfloat16 [4, 8, 56, 3, 128, 128], P('slab', 'cross'), may hold values from -0.3125 to 0.3125
- m_cols: int32 [4, 8, 56, 3], P('slab', 'cross'), may hold values from 0 to 55, as said below
- j_blocks: bfloat16 [4, 8, 32, 3, 128, 128], P('slab', 'cross'), may hold values from -0.3125 to 0.3125
- j_cols: int32 [4, 8, 32, 3], P('slab', 'cross'), may hold values from 0 to 55, as said below
- send_list: int32 [4, 8, 8, 2], P('slab', 'cross'), may hold values from 0 to 31, as said below
- send_count: int32 [4, 8, 8], P('slab', 'cross'), may hold values from 0 to 2, as said below
Outputs:
- second_iterate: bfloat16 [4, 8, 32, 128, 128], P('slab', 'cross')
Inputs may be any that keep to these rules, and one draw needn't show every extreme that they name: `m_cols`: each row's first block column is the row itself; the others differ from it and from each other. `j_cols`: each row's first block column is the row itself; the others differ from it and from each other. `send_list`: the used slots of one list name different block rows. `send_count`: no subdomain lends rows to itself; in every slab index some subdomain receives 2 rows from each other one.
All inputs are finite; a program needn't handle non-finite values.
Results may differ from a plain program's by a relative error of at most 0.0058.
Values may be sent and summed in bfloat16 or wider, within the bound.
A program may use at most 64 MiB of HBM per device.

v0:
```python
import functools

import jax
import jax.numpy as jnp
from jax import lax
from jax.experimental import pallas as pl
from jax.experimental.pallas import tpu as pltpu
from jax.sharding import PartitionSpec as P

MESH = pl.DeviceIdType.MESH
F32 = jnp.float32
BF16 = jnp.bfloat16


def kernel(
    n_slab, n, ovl,
    rhs_hbm, m_hbm, j_hbm, m_cols, j_cols, targets, counts,
    out_ref,
    m_v, j_v, own0, own1, own2, ext0, ext1, ext2, part, send_buf, ret, ret_slab, run, acc,
    prev, last, load_sem, send_sem, recv_sem,
):
    s = lax.axis_index("slab")
    c = lax.axis_index("cross")
    own = (own0, own1, own2)
    ext = (ext0, ext1, ext2)
    rows = own0.shape[0]
    cap = send_buf.shape[2]
    kcount = m_v.shape[1]
    base = rows + 2 * ovl
    slots = (n - 1) * cap
    zero_slot = slots
    up_i, down_i = n, n + 1
    has_up = s > 0
    has_down = s < n_slab - 1

    def peer(d):
        return lax.rem(c + d, n)

    def order(t):
        return n // 2 + (1 - 2 * lax.rem(t, 2)) * ((t + 1) // 2)

    load_own = pltpu.make_async_copy(rhs_hbm.at[0, 0], own0, load_sem.at[0])
    load_ext = pltpu.make_async_copy(rhs_hbm.at[0, 0], ext0.at[pl.ds(0, rows)], load_sem.at[1])
    load_m = pltpu.make_async_copy(m_hbm.at[0, 0], m_v, load_sem.at[2])
    load_j = pltpu.make_async_copy(j_hbm.at[0, 0], j_v, load_sem.at[3])
    load_own.start()
    load_ext.start()
    load_m.start()
    load_j.start()

    barrier = pltpu.get_barrier_semaphore()

    @pl.loop(1, n)
    def _(d):
        pl.semaphore_signal(barrier, inc=1, device_id=(s, peer(d)), device_id_type=MESH)

    @pl.when(has_up)
    def _():
        pl.semaphore_signal(barrier, inc=1, device_id=(s - 1, c), device_id_type=MESH)

    @pl.when(has_down)
    def _():
        pl.semaphore_signal(barrier, inc=1, device_id=(s + 1, c), device_id_type=MESH)

    zero_tile = jnp.zeros(own0.shape[1:], BF16)
    for r in range(3):
        for t in range(cap):
            ext[r][base + c * cap + t] = zero_tile

    @pl.when(jnp.logical_not(has_up))
    def _():
        for r in range(3):
            for t in range(ovl):
                ext[r][rows + t] = zero_tile
        for r in range(2):
            for t in range(ovl):
                ret_slab[r, t] = zero_tile

    @pl.when(jnp.logical_not(has_down))
    def _():
        for r in range(3):
            for t in range(ovl):
                ext[r][rows + ovl + t] = zero_tile
        for r in range(2):
            for t in range(ovl):
                ret_slab[r, ovl + t] = zero_tile

    run[zero_slot] = jnp.zeros(own0.shape[1:], F32)

    def slab_copy(src, dst, r, mine, theirs, to):
        return pltpu.make_async_remote_copy(
            src_ref=src, dst_ref=dst, send_sem=send_sem.at[r, mine], recv_sem=recv_sem.at[r, theirs],
            device_id=(to, c), device_id_type=MESH,
        )

    def lend_up(e, r):
        return slab_copy(ext[e].at[pl.ds(0, ovl)], ext[e].at[pl.ds(rows + ovl, ovl)], r, up_i, down_i, s - 1)

    def lend_down(e, r):
        return slab_copy(ext[e].at[pl.ds(rows - ovl, ovl)], ext[e].at[pl.ds(rows, ovl)], r, down_i, up_i, s + 1)

    def lend_cross(e, r, d):
        return pltpu.make_async_remote_copy(
            src_ref=send_buf.at[e, d - 1], dst_ref=ext[e].at[pl.ds(base + c * cap, cap)],
            send_sem=send_sem.at[r, d], recv_sem=recv_sem.at[r, n - d],
            device_id=(s, peer(d)), device_id_type=MESH,
        )

    def got_cross(e, r, d):
        return pltpu.make_async_remote_copy(
            src_ref=send_buf.at[e, d - 1], dst_ref=ext[e].at[pl.ds(base + peer(d) * cap, cap)],
            send_sem=send_sem.at[r, d], recv_sem=recv_sem.at[r, d],
            device_id=(s, peer(d)), device_id_type=MESH,
        )

    def got_up(e, r):
        return slab_copy(ext[e].at[pl.ds(0, ovl)], ext[e].at[pl.ds(rows, ovl)], r, up_i, up_i, s - 1)

    def got_down(e, r):
        return slab_copy(ext[e].at[pl.ds(0, ovl)], ext[e].at[pl.ds(rows + ovl, ovl)], r, down_i, down_i, s + 1)

    def lend_slab(e, r):
        @pl.when(has_up)
        def _():
            lend_up(e, r).start()

        @pl.when(has_down)
        def _():
            lend_down(e, r).start()

    def lend_rows(e, r):
        @pl.loop(0, n - 1)
        def _(step):
            d = order(step)
            q = peer(d)
            for t in range(cap):
                picked = own[e][targets[0, 0, t, q]]
                used = t < counts[0, 0, q]
                send_buf[e, d - 1, t] = jnp.where(used, picked, jnp.zeros_like(picked))
            lend_cross(e, r, d).start()

    def await_lent(e, r):
        @pl.when(has_up)
        def _():
            got_up(e, r).wait_recv()

        @pl.when(has_down)
        def _():
            got_down(e, r).wait_recv()

        @pl.loop(1, n)
        def _(d):
            got_cross(e, r, d).wait_recv()

    def finish_lend(e, r):
        @pl.when(has_up)
        def _():
            lend_up(e, r).wait_send()

        @pl.when(has_down)
        def _():
            lend_down(e, r).wait_send()

        @pl.loop(1, n)
        def _(d):
            lend_cross(e, r, d).wait_send()

    def back_up(a, r):
        return slab_copy(part.at[a, pl.ds(rows, ovl)], ret_slab.at[a, pl.ds(ovl, ovl)], r, up_i, down_i, s - 1)

    def back_down(a, r):
        return slab_copy(part.at[a, pl.ds(rows + ovl, ovl)], ret_slab.at[a, pl.ds(0, ovl)], r, down_i, up_i, s + 1)

    def home_up(a, r):
        return slab_copy(part.at[a, pl.ds(rows, ovl)], ret_slab.at[a, pl.ds(0, ovl)], r, up_i, up_i, s - 1)

    def home_down(a, r):
        return slab_copy(part.at[a, pl.ds(rows, ovl)], ret_slab.at[a, pl.ds(ovl, ovl)], r, down_i, down_i, s + 1)

    def back_cross(a, r, d):
        return pltpu.make_async_remote_copy(
            src_ref=part.at[a, pl.ds(base + peer(d) * cap, cap)], dst_ref=ret.at[a, n - d - 1],
            send_sem=send_sem.at[r, d], recv_sem=recv_sem.at[r, n - d],
            device_id=(s, peer(d)), device_id_type=MESH,
        )

    def home_cross(a, r, d):
        return pltpu.make_async_remote_copy(
            src_ref=part.at[a, pl.ds(base + peer(d) * cap, cap)], dst_ref=ret.at[a, d - 1],
            send_sem=send_sem.at[r, d], recv_sem=recv_sem.at[r, d],
            device_id=(s, peer(d)), device_id_type=MESH,
        )

    def row_product(blocks, cols, e, i, k0=0):
        left = jnp.concatenate([blocks[i, k] for k in range(k0, kcount)], axis=1)
        right = jnp.concatenate([ext[e][cols[0, k, 0, i]] for k in range(k0, kcount)], axis=0)
        return jnp.dot(left, right, preferred_element_type=F32)

    def partial_row(a, e, i):
        part[a, i] = row_product(m_v, m_cols, e, i).astype(BF16)

    def apply_and_return(a, e, r):
        @pl.loop(0, n - 1)
        def _(step):
            d = order(step)
            first_row = base + peer(d) * cap
            for t in range(cap):
                partial_row(a, e, first_row + t)
            back_cross(a, r, d).start()

        @pl.loop(0, 2 * ovl // 4)
        def _(g):
            for t in range(4):
                partial_row(a, e, rows + 4 * g + t)

        @pl.when(has_up)
        def _():
            back_up(a, r).start()

        @pl.when(has_down)
        def _():
            back_down(a, r).start()

        @pl.loop(0, rows // 4)
        def _(g):
            for t in range(4):
                partial_row(a, e, 4 * g + t)

    def await_returns(a, r):
        @pl.loop(1, n)
        def _(d):
            home_cross(a, r, d).wait_recv()
            for t in range(cap):
                p = (d - 1) * cap + t
                run[p] = ret[a, d - 1, t].astype(F32) + run[prev[p]]

        @pl.when(has_up)
        def _():
            home_up(a, r).wait_recv()

        @pl.when(has_down)
        def _():
            home_down(a, r).wait_recv()

    def finish_return(a, r):
        @pl.when(has_up)
        def _():
            back_up(a, r).wait_send()

        @pl.when(has_down)
        def _():
            back_down(a, r).wait_send()

        @pl.loop(1, n)
        def _(d):
            back_cross(a, r, d).wait_send()

    def assembled(a, body):
        def total(i):
            return part[a, i].astype(F32) + run[last[i]]

        @pl.loop(0, ovl)
        def _(t):
            i = rows - ovl + t
            body(t, total(t) + ret_slab[a, t].astype(F32))
            body(i, total(i) + ret_slab[a, ovl + t].astype(F32))

        @pl.loop(0, (rows - 2 * ovl) // 4)
        def _(g):
            for t in range(4):
                i = ovl + 4 * g + t
                body(i, total(i))

    load_own.wait()
    load_ext.wait()

    pl.semaphore_wait(barrier, n - 1 + has_up.astype(jnp.int32) + has_down.astype(jnp.int32))

    lend_slab(0, 0)
    lend_rows(0, 0)

    def key_of(p):
        q = peer(p // cap + 1)
        t = lax.rem(p, cap)
        return jnp.where(t < counts[0, 0, q], targets[0, 0, t, q], -1)

    @pl.loop(0, rows)
    def _(i):
        last[i] = zero_slot

    keys = [key_of(p) for p in range(slots)]
    for p in range(slots):
        found = zero_slot
        for p2 in range(p):
            found = jnp.where(keys[p2] == keys[p], p2, found)
        prev[p] = jnp.where(keys[p] < 0, zero_slot, found)

    @pl.loop(0, rows)
    def _(i):
        found = zero_slot
        for p in range(slots):
            found = jnp.where(keys[p] == i, p, found)
        last[i] = found

    load_m.wait()
    load_j.wait()
    await_lent(0, 0)

    apply_and_return(0, 0, 1)
    await_returns(0, 1)

    def put_first(i, value):
        rounded = value.astype(BF16)
        own[1][i] = rounded
        ext[1][i] = rounded

    assembled(0, put_first)

    lend_slab(1, 2)
    lend_rows(1, 2)

    @pl.loop(0, rows // 4)
    def _(g):
        for t in range(4):
            i = 4 * g + t
            acc[i] = own[0][i].astype(F32) - jnp.dot(j_v[i, 0], own[1][i], preferred_element_type=F32)

    await_lent(1, 2)

    @pl.loop(0, rows // 4)
    def _(g):
        for t in range(4):
            i = 4 * g + t
            rounded = (acc[i] - row_product(j_v, j_cols, 1, i, 1)).astype(BF16)
            own[2][i] = rounded
            ext[2][i] = rounded

    lend_slab(2, 3)
    lend_rows(2, 3)
    await_lent(2, 3)

    apply_and_return(1, 2, 4)
    await_returns(1, 4)

    def put_second(i, value):
        out_ref[0, 0, i] = (own[1][i].astype(F32) + value).astype(BF16)

    assembled(1, put_second)

    finish_lend(0, 0)
    finish_return(0, 1)
    finish_lend(1, 2)
    finish_lend(2, 3)
    finish_return(1, 4)


def solution(mesh):
    n_slab = mesh.shape["slab"]
    n = mesh.shape["cross"]

    def per_device(rhs, m_blocks, m_cols, j_blocks, j_cols, send_list, send_count):
        rows, blk, nv = rhs.shape[2:]
        total_rows, kcount = m_blocks.shape[2:4]
        cap = send_list.shape[3]
        ovl = (total_rows - rows - n * cap) // 2
        slots = (n - 1) * cap
        tile = (blk, nv)
        smem = pl.BlockSpec(memory_space=pltpu.SMEM)
        hbm = pl.BlockSpec(memory_space=pltpu.HBM)
        return pl.pallas_call(
            functools.partial(kernel, n_slab, n, ovl),
            out_shape=pltpu.VMEM(rhs.shape, rhs.dtype),
            in_specs=[hbm, hbm, hbm, smem, smem, smem, smem],
            out_specs=pl.BlockSpec(memory_space=pltpu.VMEM),
            scratch_shapes=[
                pltpu.VMEM(m_blocks.shape[2:], BF16),
                pltpu.VMEM(j_blocks.shape[2:], BF16),
                *([pltpu.VMEM((rows,) + tile, BF16)] * 3),
                *([pltpu.VMEM((total_rows,) + tile, BF16)] * 3),
                pltpu.VMEM((2, total_rows) + tile, BF16),
                pltpu.VMEM((3, n - 1, cap) + tile, BF16),
                pltpu.VMEM((2, n - 1, cap) + tile, BF16),
                pltpu.VMEM((2, 2 * ovl) + tile, BF16),
                pltpu.VMEM((slots + 1,) + tile, F32),
                pltpu.VMEM((rows,) + tile, F32),
                pltpu.SMEM((slots,), jnp.int32),
                pltpu.SMEM((rows,), jnp.int32),
                pltpu.SemaphoreType.DMA((4,)),
                pltpu.SemaphoreType.DMA((5, n + 2)),
                pltpu.SemaphoreType.DMA((5, n + 2)),
            ],
            compiler_params=pltpu.CompilerParams(
                collective_id=0, has_side_effects=True, vmem_limit_bytes=60 * 1024 * 1024
            ),
        )(
            rhs, m_blocks, j_blocks, m_cols.transpose(0, 3, 1, 2), j_cols.transpose(0, 3, 1, 2),
            send_list.transpose(0, 1, 3, 2), send_count,
        )

    return jax.shard_map(
        per_device,
        mesh=mesh,
        in_specs=(
            P("slab", "cross", None, None, None),
            P("slab", "cross", None, None, None, None),
            P("slab", "cross", None, None),
            P("slab", "cross", None, None, None, None),
            P("slab", "cross", None, None),
            P("slab", "cross", None, None),
            P("slab", "cross", None),
        ),
        out_specs=P("slab", "cross", None, None, None),
        check_vma=False,
    )
```

profile of v0, /device:TPU:0, one launch (start us, length us, event | category | flops | bytes accessed | tf_op | source)
XLA Modules:
  0.0 67.6 jit_solution(3953023258326947498)
XLA Ops:
  0.0 66.6 %shard_map.73 = bf16[1,1,32,128,128]{4,3,2,1,0:T(8,128)(2,1)S(1)} custom-call(bf16[1,1,32,128,128]{4,3,2,1,0:T(8,128)(2,1)} %rhs_hbm.1, bf16[1,1,56,3,128,128]{5,4,3,2,1,0:T(8,128)(2,1)} %m_hbm.1, bf16[1,1,32,3,128,128]{5,4,3,2,1,0:T(8,128)(2,1)} %j_hbm.1, s32[1,3,1,56]{3,2,1,0:T(1,128)} %bitcast.3, s32[1,3,1,32]{3,2,1,0:T(1,128)} %bitcast.4, ...), custom_call_target="tpu_custom_call" | custom-call | tf_op jit(solution)/shard_map/pallas_call | solution.py:370
  66.6 1.0 %copy.9 = bf16[1,1,32,128,128]{4,3,2,1,0:T(8,128)(2,1)} copy(bf16[1,1,32,128,128]{4,3,2,1,0:T(8,128)(2,1)S(1)} %shard_map.73) | data formatting | bytes 2097152
where the time goes:
time: 68.5 us; the launch traced here: 67.6 us
  Pallas kernels  66.6 us (97%)
  local copies, waits for them, and re-layouts  0.97 us (1%)
    pallas_call x1, Pallas kernels, per_device(): pl.pallas_call(functools.partial(kernel, n_slab, n, ovl), out_shape=pltpu...  66.6 us

commit v1 on v0

v1 whole, which is shorter than its diff:
```python
import functools

import jax
import jax.numpy as jnp
from jax import lax
from jax.experimental import pallas as pl
from jax.experimental.pallas import tpu as pltpu
from jax.sharding import PartitionSpec as P

MESH = pl.DeviceIdType.MESH
F32 = jnp.float32
BF16 = jnp.bfloat16

LENDS = 3
BACKS = 2


def kernel(
    n_slab, n, ovl, cap,
    rhs_hbm, m_hbm, j_hbm, m_cols, j_cols, targets, counts,
    out_ref,
    m_v, j_v, ext0, ext1, ext2, part, acc, run,
    lend_buf, land, lend_slab, land_slab, back_buf, ret, back_slab, ret_slab,
    prev, last, load_sem, send_sem, recv_sem,
):
    s = lax.axis_index("slab")
    c = lax.axis_index("cross")
    ext = (ext0, ext1, ext2)
    rows = part.shape[0]
    blk, nv = part.shape[1:]
    half = nv // 2
    kcount = m_v.shape[1]
    pairs = cap // 2
    opairs = ovl // 2
    base = rows + 2 * ovl
    slots = (n - 1) * cap
    zero_slot = slots
    up_i, down_i = n, n + 1
    has_up = s > 0
    has_down = s < n_slab - 1

    def peer(d):
        return lax.rem(c + d, n)

    def order(t):
        return n // 2 + (2 * lax.rem(t, 2) - 1) * ((t + 1) // 2)

    load_rhs = pltpu.make_async_copy(rhs_hbm.at[0, 0], ext0.at[pl.ds(0, rows)], load_sem.at[0])
    load_m = pltpu.make_async_copy(m_hbm.at[0, 0], m_v, load_sem.at[1])
    load_j = pltpu.make_async_copy(j_hbm.at[0, 0], j_v, load_sem.at[2])
    load_rhs.start()

    barrier = pltpu.get_barrier_semaphore()

    @pl.loop(1, n)
    def _(d):
        pl.semaphore_signal(barrier, inc=1, device_id=(s, peer(d)), device_id_type=MESH)

    @pl.when(has_up)
    def _():
        pl.semaphore_signal(barrier, inc=1, device_id=(s - 1, c), device_id_type=MESH)

    @pl.when(has_down)
    def _():
        pl.semaphore_signal(barrier, inc=1, device_id=(s + 1, c), device_id_type=MESH)

    load_m.start()
    load_j.start()


    def swap(x):
        return pltpu.roll(x, half, 1)

    def low(dtype):
        return lax.broadcasted_iota(jnp.int32, (blk, nv), 1) < half

    def pack(h, r0, r1):
        if h == 0:
            return jnp.where(low(r0.dtype), r0, swap(r1))
        return jnp.where(low(r0.dtype), swap(r0), r1)

    def apart(h, tile_of):
        a = tile_of(0)
        if h == 0:
            return a, swap(a)
        b = tile_of(1)
        mask = low(a.dtype)
        return jnp.where(mask, a, swap(b)), jnp.where(mask, swap(a), b)

    zero_tile = jnp.zeros((blk, nv), BF16)
    for e in range(LENDS):
        for t in range(cap):
            ext[e][base + c * cap + t] = zero_tile

    def clear_slab(side):
        for h in range(2):
            for u in range(opairs):
                for e in range(LENDS):
                    land_slab[e, h, side, u] = zero_tile
                for a in range(BACKS):
                    ret_slab[a, h, side, u] = zero_tile

    @pl.when(jnp.logical_not(has_up))
    def _():
        clear_slab(0)

    @pl.when(jnp.logical_not(has_down))
    def _():
        clear_slab(1)

    run[zero_slot] = jnp.zeros((blk, nv), F32)


    def cross_copy(src, dst, x, h, d):
        return pltpu.make_async_remote_copy(
            src_ref=src.at[h, d - 1], dst_ref=dst.at[h, n - d - 1],
            send_sem=send_sem.at[x, h, d], recv_sem=recv_sem.at[x, h, n - d],
            device_id=(s, peer(d)), device_id_type=MESH,
        )

    def cross_got(src, dst, x, h, d):
        return pltpu.make_async_remote_copy(
            src_ref=src.at[h, d - 1], dst_ref=dst.at[h, d - 1],
            send_sem=send_sem.at[x, h, d], recv_sem=recv_sem.at[x, h, d],
            device_id=(s, peer(d)), device_id_type=MESH,
        )

    def slab_copy(src, dst, x, h, side):
        other = 1 - side
        return pltpu.make_async_remote_copy(
            src_ref=src.at[h, side], dst_ref=dst.at[h, other],
            send_sem=send_sem.at[x, h, n + side], recv_sem=recv_sem.at[x, h, n + other],
            device_id=(s - 1 + 2 * side, c), device_id_type=MESH,
        )

    def slab_got(src, dst, x, h, side):
        return pltpu.make_async_remote_copy(
            src_ref=src.at[h, side], dst_ref=dst.at[h, side],
            send_sem=send_sem.at[x, h, n + side], recv_sem=recv_sem.at[x, h, n + side],
            device_id=(s - 1 + 2 * side, c), device_id_type=MESH,
        )

    def both_sides(do):
        @pl.when(has_up)
        def _():
            do(0)

        @pl.when(has_down)
        def _():
            do(1)

    def lend(e, h):
        src, dst = lend_buf.at[e], land.at[e]

        @pl.loop(0, n - 1)
        def _(step):
            d = order(step)
            q = peer(d)

            def picked(t):
                row = ext[e][targets[0, 0, t, q]]
                return jnp.where(t < counts[0, 0, q], row, jnp.zeros_like(row))

            for u in range(pairs):
                lend_buf[e, h, d - 1, u] = pack(h, picked(2 * u), picked(2 * u + 1))
            cross_copy(src, dst, e, h, d).start()

        for side in range(2):
            first_row = side * (rows - ovl)
            for u in range(opairs):
                r0 = first_row + 2 * u
                lend_slab[e, h, side, u] = pack(h, ext[e][r0], ext[e][r0 + 1])
        both_sides(lambda side: slab_copy(lend_slab.at[e], land_slab.at[e], e, h, side).start())

    def await_lent(e, h):
        @pl.loop(0, n - 1)
        def _(step):
            d = n - order(n - 2 - step)
            cross_got(lend_buf.at[e], land.at[e], e, h, d).wait_recv()
            for u in range(pairs):
                r0, r1 = apart(h, lambda hh: land[e, hh, d - 1, u])
                i = base + peer(d) * cap + 2 * u
                ext[e][i] = r0
                ext[e][i + 1] = r1

        both_sides(lambda side: slab_got(lend_slab.at[e], land_slab.at[e], e, h, side).wait_recv())
        for side in range(2):
            for u in range(opairs):
                r0, r1 = apart(h, lambda hh: land_slab[e, hh, side, u])
                i = rows + side * ovl + 2 * u
                ext[e][i] = r0
                ext[e][i + 1] = r1

    def row_product(blocks, cols, e, i, k0=0):
        left = jnp.concatenate([blocks[i, k] for k in range(k0, kcount)], axis=1)
        right = jnp.concatenate([ext[e][cols[0, k, 0, i]] for k in range(k0, kcount)], axis=0)
        return jnp.dot(left, right, preferred_element_type=F32)

    def give_back(a, e, h):
        x = LENDS + a

        @pl.loop(0, n - 1)
        def _(step):
            d = order(step)
            for u in range(pairs):
                i = base + peer(d) * cap + 2 * u
                tile = pack(h, row_product(m_v, m_cols, e, i), row_product(m_v, m_cols, e, i + 1))
                back_buf[a, h, d - 1, u] = tile.astype(BF16)
            cross_copy(back_buf.at[a], ret.at[a], x, h, d).start()

        for side in range(2):
            @pl.loop(0, opairs)
            def _(u):
                i = rows + side * ovl + 2 * u
                tile = pack(h, row_product(m_v, m_cols, e, i), row_product(m_v, m_cols, e, i + 1))
                back_slab[a, h, side, u] = tile.astype(BF16)

        both_sides(lambda side: slab_copy(back_slab.at[a], ret_slab.at[a], x, h, side).start())

    def own_partials(e):
        @pl.loop(0, rows // 4)
        def _(g):
            for t in range(4):
                i = 4 * g + t
                part[i] = row_product(m_v, m_cols, e, i).astype(BF16)

    def await_returns(a, h):
        x = LENDS + a

        @pl.loop(1, n)
        def _(d):
            cross_got(back_buf.at[a], ret.at[a], x, h, d).wait_recv()
            for u in range(pairs):
                two = apart(h, lambda hh: ret[a, hh, d - 1, u])
                for t in range(2):
                    p = (d - 1) * cap + 2 * u + t
                    run[p] = two[t].astype(F32) + run[prev[p]]

        both_sides(lambda side: slab_got(back_slab.at[a], ret_slab.at[a], x, h, side).wait_recv())

    def assembled(a, h, body):
        def total(i):
            return part[i].astype(F32) + run[last[i]]

        for side in range(2):
            for u in range(opairs):
                two = apart(h, lambda hh: ret_slab[a, hh, side, u])
                for t in range(2):
                    i = side * (rows - ovl) + 2 * u + t
                    body(i, total(i) + two[t].astype(F32))

        @pl.loop(0, (rows - 2 * ovl) // 4)
        def _(g):
            for t in range(4):
                i = ovl + 4 * g + t
                body(i, total(i))

    load_rhs.wait()
    pl.semaphore_wait(barrier, n - 1 + has_up.astype(jnp.int32) + has_down.astype(jnp.int32))

    lend(0, 0)
    lend(0, 1)

    def key_of(p):
        q = peer(p // cap + 1)
        t = lax.rem(p, cap)
        return jnp.where(t < counts[0, 0, q], targets[0, 0, t, q], -1)

    keys = [key_of(p) for p in range(slots)]
    for p in range(slots):
        found = zero_slot
        for p2 in range(p):
            found = jnp.where(keys[p2] == keys[p], p2, found)
        prev[p] = jnp.where(keys[p] < 0, zero_slot, found)

    @pl.loop(0, rows)
    def _(i):
        found = zero_slot
        for p in range(slots):
            found = jnp.where(keys[p] == i, p, found)
        last[i] = found

    load_m.wait()
    load_j.wait()

    await_lent(0, 0)
    give_back(0, 0, 0)
    await_lent(0, 1)
    give_back(0, 0, 1)
    own_partials(0)

    def put_first(i, value):
        ext1[i] = value.astype(BF16)

    for h in range(2):
        await_returns(0, h)
        assembled(0, h, put_first)
        lend(1, h)

    @pl.loop(0, rows // 4)
    def _(g):
        for t in range(4):
            i = 4 * g + t
            acc[i] = ext0[i].astype(F32) - jnp.dot(j_v[i, 0], ext1[i], preferred_element_type=F32)

    for h in range(2):
        await_lent(1, h)

        @pl.loop(0, rows // 4)
        def _(g):
            for t in range(4):
                i = 4 * g + t
                ext2[i] = (acc[i] - row_product(j_v, j_cols, 1, i, 1)).astype(BF16)

        lend(2, h)

    for h in range(2):
        await_lent(2, h)
        give_back(1, 2, h)

    own_partials(2)

    def put_second(i, value):
        out_ref[0, 0, i] = (ext1[i].astype(F32) + value).astype(BF16)

    both_sides(lambda side: slab_got(back_slab.at[1], ret_slab.at[1], LENDS + 1, 0, side).wait_recv())

    @pl.loop(1, n)
    def _(d):
        cross_got(back_buf.at[1], ret.at[1], LENDS + 1, 0, d).wait_recv()

    await_returns(1, 1)
    assembled(1, 1, put_second)

    for h in range(2):
        for e in range(LENDS):
            @pl.loop(1, n)
            def _(d):
                cross_copy(lend_buf.at[e], land.at[e], e, h, d).wait_send()

            both_sides(lambda side: slab_copy(lend_slab.at[e], land_slab.at[e], e, h, side).wait_send())
        for a in range(BACKS):
            @pl.loop(1, n)
            def _(d):
                cross_copy(back_buf.at[a], ret.at[a], LENDS + a, h, d).wait_send()

            both_sides(lambda side: slab_copy(back_slab.at[a], ret_slab.at[a], LENDS + a, h, side).wait_send())


def solution(mesh):
    n_slab = mesh.shape["slab"]
    n = mesh.shape["cross"]

    def per_device(rhs, m_blocks, m_cols, j_blocks, j_cols, send_list, send_count):
        rows, blk, nv = rhs.shape[2:]
        total_rows, kcount = m_blocks.shape[2:4]
        cap = send_list.shape[3]
        ovl = (total_rows - rows - n * cap) // 2
        slots = (n - 1) * cap
        tile = (blk, nv)
        smem = pl.BlockSpec(memory_space=pltpu.SMEM)
        hbm = pl.BlockSpec(memory_space=pltpu.HBM)
        return pl.pallas_call(
            functools.partial(kernel, n_slab, n, ovl, cap),
            out_shape=pltpu.VMEM(rhs.shape, rhs.dtype),
            in_specs=[hbm, hbm, hbm, smem, smem, smem, smem],
            out_specs=pl.BlockSpec(memory_space=pltpu.VMEM),
            scratch_shapes=[
                pltpu.VMEM(m_blocks.shape[2:], BF16),
                pltpu.VMEM(j_blocks.shape[2:], BF16),
                *([pltpu.VMEM((total_rows,) + tile, BF16)] * LENDS),
                pltpu.VMEM((rows,) + tile, BF16),
                pltpu.VMEM((rows,) + tile, F32),
                pltpu.VMEM((slots + 1,) + tile, F32),
                *([pltpu.VMEM((LENDS, 2, n - 1, cap // 2) + tile, BF16)] * 2),
                *([pltpu.VMEM((LENDS, 2, 2, ovl // 2) + tile, BF16)] * 2),
                *([pltpu.VMEM((BACKS, 2, n - 1, cap // 2) + tile, BF16)] * 2),
                *([pltpu.VMEM((BACKS, 2, 2, ovl // 2) + tile, BF16)] * 2),
                pltpu.SMEM((slots,), jnp.int32),
                pltpu.SMEM((rows,), jnp.int32),
                pltpu.SemaphoreType.DMA((3,)),
                pltpu.SemaphoreType.DMA((LENDS + BACKS, 2, n + 2)),
                pltpu.SemaphoreType.DMA((LENDS + BACKS, 2, n + 2)),
            ],
            compiler_params=pltpu.CompilerParams(
                collective_id=0, has_side_effects=True, vmem_limit_bytes=60 * 1024 * 1024
            ),
        )(
            rhs, m_blocks, j_blocks, m_cols.transpose(0, 3, 1, 2), j_cols.transpose(0, 3, 1, 2),
            send_list.transpose(0, 1, 3, 2), send_count,
        )

    return jax.shard_map(
        per_device,
        mesh=mesh,
        in_specs=(
            P("slab", "cross", None, None, None),
            P("slab", "cross", None, None, None, None),
            P("slab", "cross", None, None),
            P("slab", "cross", None, None, None, None),
            P("slab", "cross", None, None),
            P("slab", "cross", None, None),
            P("slab", "cross", None),
        ),
        out_specs=P("slab", "cross", None, None, None),
        check_vma=False,
    )
```

time: 68.5 us -> 68.6 us (level)
  Pallas kernels: 66.6 us -> 67.4 us
    pallas_call x1, Pallas kernels: 66.6 us -> 67.4 us  [per_device(): pl.pallas_call(functools.partial(kernel, n_slab, n, ovl, cap), out_shape=...]
where the time goes in v1:
time: 68.6 us; the launch traced here: 68.3 us
  Pallas kernels  67.4 us (98%)
  local copies, waits for them, and re-layouts  0.97 us (1%)
    pallas_call x1, Pallas kernels, per_device(): pl.pallas_call(functools.partial(kernel, n_slab, n, ovl, cap), out_shape=...  67.4 us

profile of v1, /device:TPU:0, one launch (start us, length us, event | category | flops | bytes accessed | tf_op | source)
XLA Modules:
  0.0 68.3 jit_solution(169200842430548971)
XLA Ops:
  0.0 67.4 %shard_map.73 = bf16[1,1,32,128,128]{4,3,2,1,0:T(8,128)(2,1)S(1)} custom-call(bf16[1,1,32,128,128]{4,3,2,1,0:T(8,128)(2,1)} %rhs_hbm.1, bf16[1,1,56,3,128,128]{5,4,3,2,1,0:T(8,128)(2,1)} %m_hbm.1, bf16[1,1,32,3,128,128]{5,4,3,2,1,0:T(8,128)(2,1)} %j_hbm.1, s32[1,3,1,56]{3,2,1,0:T(1,128)} %bitcast.3, s32[1,3,1,32]{3,2,1,0:T(1,128)} %bitcast.4, ...), custom_call_target="tpu_custom_call" | custom-call | tf_op jit(solution)/shard_map/pallas_call | solution.py:363
  67.4 1.0 %copy.9 = bf16[1,1,32,128,128]{4,3,2,1,0:T(8,128)(2,1)} copy(bf16[1,1,32,128,128]{4,3,2,1,0:T(8,128)(2,1)S(1)} %shard_map.73) | data formatting | bytes 2097152

commit v2 on v1

--- a/solution.py
+++ b/solution.py
@@ -39,11 +39,29 @@
     has_up = s > 0
     has_down = s < n_slab - 1
 
+    paired = n & (n - 1) == 0
+    centre = jnp.logical_and(c >= n // 4, c < n - n // 4)
+    shift = jnp.where(centre, n // 2 - 1, 0)
+
     def peer(d):
-        return lax.rem(c + d, n)
+        return jnp.bitwise_xor(c, d) if paired else lax.rem(c + d, n)
+
+    def mirror(d):
+        return d if paired else n - d
 
     def order(t):
-        return n // 2 + (2 * lax.rem(t, 2) - 1) * ((t + 1) // 2)
+        return lax.rem(t + shift, n - 1) + 1
+
+    def grouped(do):
+        do([0])
+        pairs_of = (n - 2) // 2
+
+        @pl.loop(0, pairs_of)
+        def _(g):
+            do([1 + 2 * g, 2 + 2 * g])
+
+        for t in range(1 + 2 * pairs_of, n - 1):
+            do([t])
 
     load_rhs = pltpu.make_async_copy(rhs_hbm.at[0, 0], ext0.at[pl.ds(0, rows)], load_sem.at[0])
     load_m = pltpu.make_async_copy(m_hbm.at[0, 0], m_v, load_sem.at[1])
@@ -87,41 +105,25 @@
         mask = low(a.dtype)
         return jnp.where(mask, a, swap(b)), jnp.where(mask, swap(a), b)
 
-    zero_tile = jnp.zeros((blk, nv), BF16)
-    for e in range(LENDS):
-        for t in range(cap):
-            ext[e][base + c * cap + t] = zero_tile
-
-    def clear_slab(side):
-        for h in range(2):
-            for u in range(opairs):
-                for e in range(LENDS):
-                    land_slab[e, h, side, u] = zero_tile
-                for a in range(BACKS):
-                    ret_slab[a, h, side, u] = zero_tile
-
-    @pl.when(jnp.logical_not(has_up))
-    def _():
-        clear_slab(0)
-
-    @pl.when(jnp.logical_not(has_down))
-    def _():
-        clear_slab(1)
-
-    run[zero_slot] = jnp.zeros((blk, nv), F32)
-
 
     def cross_copy(src, dst, x, h, d):
         return pltpu.make_async_remote_copy(
-            src_ref=src.at[h, d - 1], dst_ref=dst.at[h, n - d - 1],
-            send_sem=send_sem.at[x, h, d], recv_sem=recv_sem.at[x, h, n - d],
+            src_ref=src.at[h, d - 1], dst_ref=dst.at[h, mirror(d) - 1],
+            send_sem=send_sem.at[x, h, 0], recv_sem=recv_sem.at[x, h, 0 if x < LENDS else mirror(d)],
             device_id=(s, peer(d)), device_id_type=MESH,
+        )
+
+    def cross_all(src, dst, x, h):
+        return pltpu.make_async_remote_copy(
+            src_ref=src.at[h], dst_ref=dst.at[h],
+            send_sem=send_sem.at[x, h, 0], recv_sem=recv_sem.at[x, h, 0],
+            device_id=(s, peer(1)), device_id_type=MESH,
         )
 
     def cross_got(src, dst, x, h, d):
         return pltpu.make_async_remote_copy(
             src_ref=src.at[h, d - 1], dst_ref=dst.at[h, d - 1],
-            send_sem=send_sem.at[x, h, d], recv_sem=recv_sem.at[x, h, d],
+            send_sem=send_sem.at[x, h, 0], recv_sem=recv_sem.at[x, h, d],
             device_id=(s, peer(d)), device_id_type=MESH,
         )
 
@@ -149,40 +151,39 @@
         def _():
             do(1)
 
-    def lend(e, h):
-        src, dst = lend_buf.at[e], land.at[e]
-
-        @pl.loop(0, n - 1)
-        def _(step):
-            d = order(step)
-            q = peer(d)
-
-            def picked(t):
-                row = ext[e][targets[0, 0, t, q]]
-                return jnp.where(t < counts[0, 0, q], row, jnp.zeros_like(row))
-
-            for u in range(pairs):
-                lend_buf[e, h, d - 1, u] = pack(h, picked(2 * u), picked(2 * u + 1))
-            cross_copy(src, dst, e, h, d).start()
-
+    def pack_lent(e, h, d):
+        q = peer(d)
+
+        def picked(t):
+            row = ext[e][targets[0, 0, t, q]]
+            return jnp.where(t < counts[0, 0, q], row, jnp.zeros_like(row))
+
+        for u in range(pairs):
+            lend_buf[e, h, d - 1, u] = pack(h, picked(2 * u), picked(2 * u + 1))
+
+    def pack_slab(e, h):
         for side in range(2):
             first_row = side * (rows - ovl)
             for u in range(opairs):
                 r0 = first_row + 2 * u
                 lend_slab[e, h, side, u] = pack(h, ext[e][r0], ext[e][r0 + 1])
+
+    def send_slab(e, h):
         both_sides(lambda side: slab_copy(lend_slab.at[e], land_slab.at[e], e, h, side).start())
 
+    def lend(e, h):
+        def some(steps):
+            ds = [order(t) for t in steps]
+            for d in ds:
+                pack_lent(e, h, d)
+            for d in ds:
+                cross_copy(lend_buf.at[e], land.at[e], e, h, d).start()
+
+        grouped(some)
+        pack_slab(e, h)
+        send_slab(e, h)
+
     def await_lent(e, h):
-        @pl.loop(0, n - 1)
-        def _(step):
-            d = n - order(n - 2 - step)
-            cross_got(lend_buf.at[e], land.at[e], e, h, d).wait_recv()
-            for u in range(pairs):
-                r0, r1 = apart(h, lambda hh: land[e, hh, d - 1, u])
-                i = base + peer(d) * cap + 2 * u
-                ext[e][i] = r0
-                ext[e][i + 1] = r1
-
         both_sides(lambda side: slab_got(lend_slab.at[e], land_slab.at[e], e, h, side).wait_recv())
         for side in range(2):
             for u in range(opairs):
@@ -190,38 +191,52 @@
                 i = rows + side * ovl + 2 * u
                 ext[e][i] = r0
                 ext[e][i + 1] = r1
+        cross_all(lend_buf.at[e], land.at[e], e, h).wait_recv()
+
+        def some(steps):
+            for t in steps:
+                d = t + 1
+                for u in range(pairs):
+                    r0, r1 = apart(h, lambda hh: land[e, hh, d - 1, u])
+                    i = base + peer(d) * cap + 2 * u
+                    ext[e][i] = r0
+                    ext[e][i + 1] = r1
+
+        grouped(some)
 
     def row_product(blocks, cols, e, i, k0=0):
         left = jnp.concatenate([blocks[i, k] for k in range(k0, kcount)], axis=1)
         right = jnp.concatenate([ext[e][cols[0, k, 0, i]] for k in range(k0, kcount)], axis=0)
         return jnp.dot(left, right, preferred_element_type=F32)
 
+    def packed_product(a, e, h, i):
+        return pack(h, row_product(m_v, m_cols, e, i), row_product(m_v, m_cols, e, i + 1)).astype(BF16)
+
     def give_back(a, e, h):
         x = LENDS + a
 
-        @pl.loop(0, n - 1)
-        def _(step):
-            d = order(step)
-            for u in range(pairs):
-                i = base + peer(d) * cap + 2 * u
-                tile = pack(h, row_product(m_v, m_cols, e, i), row_product(m_v, m_cols, e, i + 1))
-                back_buf[a, h, d - 1, u] = tile.astype(BF16)
-            cross_copy(back_buf.at[a], ret.at[a], x, h, d).start()
-
-        for side in range(2):
-            @pl.loop(0, opairs)
-            def _(u):
-                i = rows + side * ovl + 2 * u
-                tile = pack(h, row_product(m_v, m_cols, e, i), row_product(m_v, m_cols, e, i + 1))
-                back_slab[a, h, side, u] = tile.astype(BF16)
+        def some(steps):
+            ds = [order(t) for t in steps]
+            for d in ds:
+                for u in range(pairs):
+                    back_buf[a, h, d - 1, u] = packed_product(a, e, h, base + peer(d) * cap + 2 * u)
+            for d in ds:
+                cross_copy(back_buf.at[a], ret.at[a], x, h, d).start()
+
+        grouped(some)
+
+        @pl.loop(0, 2)
+        def _(side):
+            for u in range(opairs):
+                back_slab[a, h, side, u] = packed_product(a, e, h, rows + side * ovl + 2 * u)
 
         both_sides(lambda side: slab_copy(back_slab.at[a], ret_slab.at[a], x, h, side).start())
 
     def own_partials(e):
-        @pl.loop(0, rows // 4)
+        @pl.loop(0, rows // 8)
         def _(g):
-            for t in range(4):
-                i = 4 * g + t
+            for t in range(8):
+                i = 8 * g + t
                 part[i] = row_product(m_v, m_cols, e, i).astype(BF16)
 
     def await_returns(a, h):
@@ -261,6 +276,29 @@
     lend(0, 0)
     lend(0, 1)
 
+    zero_tile = jnp.zeros((blk, nv), BF16)
+    for e in range(LENDS):
+        for t in range(cap):
+            ext[e][base + c * cap + t] = zero_tile
+
+    def clear_slab(side):
+        for h in range(2):
+            for u in range(opairs):
+                for e in range(LENDS):
+                    land_slab[e, h, side, u] = zero_tile
+                for a in range(BACKS):
+                    ret_slab[a, h, side, u] = zero_tile
+
+    @pl.when(jnp.logical_not(has_up))
+    def _():
+        clear_slab(0)
+
+    @pl.when(jnp.logical_not(has_down))
+    def _():
+        clear_slab(1)
+
+    run[zero_slot] = jnp.zeros((blk, nv), F32)
+
     def key_of(p):
         q = peer(p // cap + 1)
         t = lax.rem(p, cap)
@@ -297,19 +335,19 @@
         assembled(0, h, put_first)
         lend(1, h)
 
-    @pl.loop(0, rows // 4)
+    @pl.loop(0, rows // 16)
     def _(g):
-        for t in range(4):
-            i = 4 * g + t
+        for t in range(16):
+            i = 16 * g + t
             acc[i] = ext0[i].astype(F32) - jnp.dot(j_v[i, 0], ext1[i], preferred_element_type=F32)
 
     for h in range(2):
         await_lent(1, h)
 
-        @pl.loop(0, rows // 4)
+        @pl.loop(0, rows // 16)
         def _(g):
-            for t in range(4):
-                i = 4 * g + t
+            for t in range(16):
+                i = 16 * g + t
                 ext2[i] = (acc[i] - row_product(j_v, j_cols, 1, i, 1)).astype(BF16)
 
         lend(2, h)
@@ -323,6 +361,16 @@
     def put_second(i, value):
         out_ref[0, 0, i] = (ext1[i].astype(F32) + value).astype(BF16)
 
+    def sent(src, dst, src_slab, dst_slab, x, h):
+        cross_all(src, dst, x, h).wait_send()
+        both_sides(lambda side: slab_copy(src_slab, dst_slab, x, h, side).wait_send())
+
+    for h in range(2):
+        for e in range(LENDS):
+            sent(lend_buf.at[e], land.at[e], lend_slab.at[e], land_slab.at[e], e, h)
+        for a in range(BACKS):
+            sent(back_buf.at[a], ret.at[a], back_slab.at[a], ret_slab.at[a], LENDS + a, h)
+
     both_sides(lambda side: slab_got(back_slab.at[1], ret_slab.at[1], LENDS + 1, 0, side).wait_recv())
 
     @pl.loop(1, n)
@@ -331,20 +379,6 @@
 
     await_returns(1, 1)
     assembled(1, 1, put_second)
-
-    for h in range(2):
-        for e in range(LENDS):
-            @pl.loop(1, n)
-            def _(d):
-                cross_copy(lend_buf.at[e], land.at[e], e, h, d).wait_send()
-
-            both_sides(lambda side: slab_copy(lend_slab.at[e], land_slab.at[e], e, h, side).wait_send())
-        for a in range(BACKS):
-            @pl.loop(1, n)
-            def _(d):
-                cross_copy(back_buf.at[a], ret.at[a], LENDS + a, h, d).wait_send()
-
-            both_sides(lambda side: slab_copy(back_slab.at[a], ret_slab.at[a], LENDS + a, h, side).wait_send())
 
 
 def solution(mesh):

time: 68.6 us -> 67 us (0.977)
  Pallas kernels: 67.4 us -> 65.8 us
    pallas_call x1, Pallas kernels: 67.4 us -> 65.8 us  [per_device(): pl.pallas_call(functools.partial(kernel, n_slab, n, ovl, cap), out_shape=...]
where the time goes in v2:
time: 67 us; the launch traced here: 66.8 us
  Pallas kernels  65.8 us (98%)
  local copies, waits for them, and re-layouts  0.97 us (1%)
    pallas_call x1, Pallas kernels, per_device(): pl.pallas_call(functools.partial(kernel, n_slab, n, ovl, cap), out_shape=...  65.8 us

profile of v2, /device:TPU:0, one launch (start us, length us, event | category | flops | bytes accessed | tf_op | source)
XLA Modules:
  0.0 66.8 jit_solution(6499820931424502419)
XLA Ops:
  0.0 65.8 %shard_map.73 = bf16[1,1,32,128,128]{4,3,2,1,0:T(8,128)(2,1)S(1)} custom-call(bf16[1,1,32,128,128]{4,3,2,1,0:T(8,128)(2,1)} %rhs_hbm.1, bf16[1,1,56,3,128,128]{5,4,3,2,1,0:T(8,128)(2,1)} %m_hbm.1, bf16[1,1,32,3,128,128]{5,4,3,2,1,0:T(8,128)(2,1)} %j_hbm.1, s32[1,3,1,56]{3,2,1,0:T(1,128)} %bitcast.3, s32[1,3,1,32]{3,2,1,0:T(1,128)} %bitcast.4, ...), custom_call_target="tpu_custom_call" | custom-call | tf_op jit(solution)/shard_map/pallas_call | solution.py:397
  65.8 1.0 %copy.9 = bf16[1,1,32,128,128]{4,3,2,1,0:T(8,128)(2,1)} copy(bf16[1,1,32,128,128]{4,3,2,1,0:T(8,128)(2,1)S(1)} %shard_map.73) | data formatting | bytes 2097152

commit v3 on v2

--- a/solution.py
+++ b/solution.py
@@ -21,7 +21,7 @@
     out_ref,
     m_v, j_v, ext0, ext1, ext2, part, acc, run,
     lend_buf, land, lend_slab, land_slab, back_buf, ret, back_slab, ret_slab,
-    prev, last, load_sem, send_sem, recv_sem,
+    prev, last, load_sem, send_sem, recv_sem, ends_in, rest_in, down_in,
 ):
     s = lax.axis_index("slab")
     c = lax.axis_index("cross")
@@ -39,15 +39,12 @@
     has_up = s > 0
     has_down = s < n_slab - 1
 
-    paired = n & (n - 1) == 0
+    assert n >= 4 and n & (n - 1) == 0
     centre = jnp.logical_and(c >= n // 4, c < n - n // 4)
     shift = jnp.where(centre, n // 2 - 1, 0)
 
     def peer(d):
-        return jnp.bitwise_xor(c, d) if paired else lax.rem(c + d, n)
-
-    def mirror(d):
-        return d if paired else n - d
+        return jnp.bitwise_xor(c, d)
 
     def order(t):
         return lax.rem(t + shift, n - 1) + 1
@@ -70,17 +67,40 @@
 
     barrier = pltpu.get_barrier_semaphore()
 
-    @pl.loop(1, n)
-    def _(d):
-        pl.semaphore_signal(barrier, inc=1, device_id=(s, peer(d)), device_id_type=MESH)
-
-    @pl.when(has_up)
-    def _():
-        pl.semaphore_signal(barrier, inc=1, device_id=(s - 1, c), device_id_type=MESH)
+    def greet(sem, to_slab, to_cross):
+        pl.semaphore_signal(sem, inc=1, device_id=(to_slab, to_cross), device_id_type=MESH)
+
+    quarter = n // 4
+    centre_first = quarter
+    centre_count = n // 2
+
+    @pl.when(centre)
+    def _():
+        @pl.loop(1, n)
+        def _(d):
+            greet(barrier, s, lax.rem(c + d, n))
 
     @pl.when(has_down)
     def _():
-        pl.semaphore_signal(barrier, inc=1, device_id=(s + 1, c), device_id_type=MESH)
+        greet(barrier, s + 1, c)
+
+    def pass_barrier():
+        expected = centre_count - centre.astype(jnp.int32) + has_up.astype(jnp.int32)
+        pl.semaphore_wait(barrier, expected)
+
+        @pl.when(jnp.logical_not(centre))
+        def _():
+            @pl.loop(centre_first, centre_first + centre_count)
+            def _(q):
+                greet(ends_in, s, q)
+
+        @pl.when(has_up)
+        def _():
+            greet(down_in, s - 1, c)
+
+    def hear_ends():
+        pl.semaphore_wait(ends_in, n - centre_count)
+        greet(rest_in, s, jnp.where(c < n // 2, c - quarter, c + quarter))
 
     load_m.start()
     load_j.start()
@@ -108,8 +128,8 @@
 
     def cross_copy(src, dst, x, h, d):
         return pltpu.make_async_remote_copy(
-            src_ref=src.at[h, d - 1], dst_ref=dst.at[h, mirror(d) - 1],
-            send_sem=send_sem.at[x, h, 0], recv_sem=recv_sem.at[x, h, 0 if x < LENDS else mirror(d)],
+            src_ref=src.at[h, d - 1], dst_ref=dst.at[h, d - 1],
+            send_sem=send_sem.at[x, h, 0], recv_sem=recv_sem.at[x, h, 0 if x < LENDS else d],
             device_id=(s, peer(d)), device_id_type=MESH,
         )
 
@@ -271,10 +291,40 @@
                 body(i, total(i))
 
     load_rhs.wait()
-    pl.semaphore_wait(barrier, n - 1 + has_up.astype(jnp.int32) + has_down.astype(jnp.int32))
-
-    lend(0, 0)
-    lend(0, 1)
+    pass_barrier()
+
+    def lend_some(h, low_d, high_d):
+        @pl.loop(low_d, high_d)
+        def _(d):
+            pack_lent(0, h, d)
+            cross_copy(lend_buf.at[0], land.at[0], 0, h, d).start()
+
+
+    @pl.when(centre)
+    def _():
+        lend_some(0, 3 * quarter, n)
+        lend_some(1, 3 * quarter, n)
+        hear_ends()
+        for h in range(2):
+            lend_some(h, 2 * quarter, 3 * quarter)
+            lend_some(h, 1, 2 * quarter)
+
+    @pl.when(jnp.logical_not(centre))
+    def _():
+        lend_some(0, quarter, 3 * quarter)
+        pl.semaphore_wait(rest_in, 1)
+        lend_some(0, 3 * quarter, n)
+        lend_some(0, 1, quarter)
+        lend_some(1, quarter, n)
+        lend_some(1, 1, quarter)
+
+    @pl.when(has_down)
+    def _():
+        pl.semaphore_wait(down_in, 1)
+
+    for h in range(2):
+        pack_slab(0, h)
+        send_slab(0, h)
 
     zero_tile = jnp.zeros((blk, nv), BF16)
     for e in range(LENDS):
@@ -415,6 +465,9 @@
                 pltpu.SemaphoreType.DMA((3,)),
                 pltpu.SemaphoreType.DMA((LENDS + BACKS, 2, n + 2)),
                 pltpu.SemaphoreType.DMA((LENDS + BACKS, 2, n + 2)),
+                pltpu.SemaphoreType.REGULAR,
+                pltpu.SemaphoreType.REGULAR,
+                pltpu.SemaphoreType.REGULAR,
             ],
             compiler_params=pltpu.CompilerParams(
                 collective_id=0, has_side_effects=True, vmem_limit_bytes=60 * 1024 * 1024

time: 67 us -> 65.4 us (0.976)
  Pallas kernels: 65.8 us -> 64.2 us
    pallas_call x1, Pallas kernels: 65.8 us -> 64.2 us  [per_device(): pl.pallas_call(functools.partial(kernel, n_slab, n, ovl, cap), out_shape=...]
where the time goes in v3:
time: 65.4 us; the launch traced here: 65.2 us
  Pallas kernels  64.2 us (98%)
  local copies, waits for them, and re-layouts  0.97 us (1%)
    pallas_call x1, Pallas kernels, per_device(): pl.pallas_call(functools.partial(kernel, n_slab, n, ovl, cap), out_shape=...  64.2 us

profile of v3, /device:TPU:0, one launch (start us, length us, event | category | flops | bytes accessed | tf_op | source)
XLA Modules:
  0.0 65.2 jit_solution(3631795844705352364)
XLA Ops:
  0.0 64.2 %shard_map.73 = bf16[1,1,32,128,128]{4,3,2,1,0:T(8,128)(2,1)S(1)} custom-call(bf16[1,1,32,128,128]{4,3,2,1,0:T(8,128)(2,1)} %rhs_hbm.1, bf16[1,1,56,3,128,128]{5,4,3,2,1,0:T(8,128)(2,1)} %m_hbm.1, bf16[1,1,32,3,128,128]{5,4,3,2,1,0:T(8,128)(2,1)} %j_hbm.1, s32[1,3,1,56]{3,2,1,0:T(1,128)} %bitcast.3, s32[1,3,1,32]{3,2,1,0:T(1,128)} %bitcast.4, ...), custom_call_target="tpu_custom_call" | custom-call | tf_op jit(solution)/shard_map/pallas_call | solution.py:447
  64.2 1.0 %copy.9 = bf16[1,1,32,128,128]{4,3,2,1,0:T(8,128)(2,1)} copy(bf16[1,1,32,128,128]{4,3,2,1,0:T(8,128)(2,1)S(1)} %shard_map.73) | data formatting | bytes 2097152

commit v4 on v3

--- a/solution.py
+++ b/solution.py
@@ -46,8 +46,10 @@
     def peer(d):
         return jnp.bitwise_xor(c, d)
 
-    def order(t):
+    def order(t, shift=shift):
         return lax.rem(t + shift, n - 1) + 1
+
+    last_shift = jnp.where(centre, 2 * (n // 4) - 1, 3 * (n // 4) - 1)
 
     def grouped(do):
         do([0])
@@ -101,9 +103,6 @@
     def hear_ends():
         pl.semaphore_wait(ends_in, n - centre_count)
         greet(rest_in, s, jnp.where(c < n // 2, c - quarter, c + quarter))
-
-    load_m.start()
-    load_j.start()
 
 
     def swap(x):
@@ -236,7 +235,7 @@
         x = LENDS + a
 
         def some(steps):
-            ds = [order(t) for t in steps]
+            ds = [order(t, last_shift if a == 1 else shift) for t in steps]
             for d in ds:
                 for u in range(pairs):
                     back_buf[a, h, d - 1, u] = packed_product(a, e, h, base + peer(d) * cap + 2 * u)
@@ -259,7 +258,7 @@
                 i = 8 * g + t
                 part[i] = row_product(m_v, m_cols, e, i).astype(BF16)
 
-    def await_returns(a, h):
+    def chain_returns(a, h):
         x = LENDS + a
 
         @pl.loop(1, n)
@@ -271,7 +270,9 @@
                     p = (d - 1) * cap + 2 * u + t
                     run[p] = two[t].astype(F32) + run[prev[p]]
 
-        both_sides(lambda side: slab_got(back_slab.at[a], ret_slab.at[a], x, h, side).wait_recv())
+    def await_returns(a, h):
+        chain_returns(a, h)
+        both_sides(lambda side: slab_got(back_slab.at[a], ret_slab.at[a], LENDS + a, h, side).wait_recv())
 
     def assembled(a, h, body):
         def total(i):
@@ -290,8 +291,10 @@
                 i = ovl + 4 * g + t
                 body(i, total(i))
 
+    pass_barrier()
     load_rhs.wait()
-    pass_barrier()
+    load_m.start()
+    load_j.start()
 
     def lend_some(h, low_d, high_d):
         @pl.loop(low_d, high_d)
@@ -408,9 +411,6 @@
 
     own_partials(2)
 
-    def put_second(i, value):
-        out_ref[0, 0, i] = (ext1[i].astype(F32) + value).astype(BF16)
-
     def sent(src, dst, src_slab, dst_slab, x, h):
         cross_all(src, dst, x, h).wait_send()
         both_sides(lambda side: slab_copy(src_slab, dst_slab, x, h, side).wait_send())
@@ -421,14 +421,33 @@
         for a in range(BACKS):
             sent(back_buf.at[a], ret.at[a], back_slab.at[a], ret_slab.at[a], LENDS + a, h)
 
-    both_sides(lambda side: slab_got(back_slab.at[1], ret_slab.at[1], LENDS + 1, 0, side).wait_recv())
+
+    @pl.loop(0, rows // 4)
+    def _(g):
+        for t in range(4):
+            i = 4 * g + t
+            acc[i] = ext1[i].astype(F32) + part[i].astype(F32)
+
+    for h in range(2):
+        both_sides(lambda side: slab_got(back_slab.at[1], ret_slab.at[1], LENDS + 1, h, side).wait_recv())
+    for side in range(2):
+        for u in range(opairs):
+            two = apart(1, lambda hh: ret_slab[1, hh, side, u])
+            for t in range(2):
+                i = side * (rows - ovl) + 2 * u + t
+                acc[i] = acc[i] + two[t].astype(F32)
 
     @pl.loop(1, n)
     def _(d):
         cross_got(back_buf.at[1], ret.at[1], LENDS + 1, 0, d).wait_recv()
 
-    await_returns(1, 1)
-    assembled(1, 1, put_second)
+    chain_returns(1, 1)
+
+    @pl.loop(0, rows // 8)
+    def _(g):
+        for t in range(8):
+            i = 8 * g + t
+            out_ref[0, 0, i] = (acc[i] + run[last[i]]).astype(BF16)
 
 
 def solution(mesh):

time: 65.4 us -> 64.8 us (level)
  no operation moved by 1% of the time
where the time goes in v4:
time: 64.8 us; the launch traced here: 64.6 us
  Pallas kernels  63.6 us (98%)
  local copies, waits for them, and re-layouts  0.97 us (1%)
    pallas_call x1, Pallas kernels, per_device(): pl.pallas_call(functools.partial(kernel, n_slab, n, ovl, cap), out_shape=...  63.6 us

profile of v4, /device:TPU:0, one launch (start us, length us, event | category | flops | bytes accessed | tf_op | source)
XLA Modules:
  0.0 64.6 jit_solution(14386550703421504854)
XLA Ops:
  0.0 63.6 %shard_map.73 = bf16[1,1,32,128,128]{4,3,2,1,0:T(8,128)(2,1)S(1)} custom-call(bf16[1,1,32,128,128]{4,3,2,1,0:T(8,128)(2,1)} %rhs_hbm.1, bf16[1,1,56,3,128,128]{5,4,3,2,1,0:T(8,128)(2,1)} %m_hbm.1, bf16[1,1,32,3,128,128]{5,4,3,2,1,0:T(8,128)(2,1)} %j_hbm.1, s32[1,3,1,56]{3,2,1,0:T(1,128)} %bitcast.3, s32[1,3,1,32]{3,2,1,0:T(1,128)} %bitcast.4, ...), custom_call_target="tpu_custom_call" | custom-call | tf_op jit(solution)/shard_map/pallas_call | solution.py:466
  63.6 1.0 %copy.9 = bf16[1,1,32,128,128]{4,3,2,1,0:T(8,128)(2,1)} copy(bf16[1,1,32,128,128]{4,3,2,1,0:T(8,128)(2,1)S(1)} %shard_map.73) | data formatting | bytes 2097152

commit v5 on v4

--- a/solution.py
+++ b/solution.py
@@ -18,10 +18,10 @@
 def kernel(
     n_slab, n, ovl, cap,
     rhs_hbm, m_hbm, j_hbm, m_cols, j_cols, targets, counts,
-    out_ref,
-    m_v, j_v, ext0, ext1, ext2, part, acc, run,
+    acc, run, last,
+    m_v, j_v, ext0, ext1, ext2, part,
     lend_buf, land, lend_slab, land_slab, back_buf, ret, back_slab, ret_slab,
-    prev, last, load_sem, send_sem, recv_sem, ends_in, rest_in, down_in,
+    prev, load_sem, send_sem, recv_sem, ends_in, rest_in, down_in,
 ):
     s = lax.axis_index("slab")
     c = lax.axis_index("cross")
@@ -443,11 +443,21 @@
 
     chain_returns(1, 1)
 
-    @pl.loop(0, rows // 8)
-    def _(g):
-        for t in range(8):
-            i = 8 * g + t
-            out_ref[0, 0, i] = (acc[i] + run[last[i]]).astype(BF16)
+
+def finish(parts, acc, run, last, out_hbm, out_v, sems):
+    share = out_v.shape[0] // parts
+
+    def write(g):
+        some = pl.ds(g * share, share)
+        return pltpu.make_async_copy(out_v.at[some], out_hbm.at[0, 0, some], sems.at[g])
+
+    for g in range(parts):
+        for t in range(share):
+            i = g * share + t
+            out_v[i] = (acc[i] + run[last[i]]).astype(BF16)
+        write(g).start()
+    for g in range(parts):
+        write(g).wait()
 
 
 def solution(mesh):
@@ -463,24 +473,26 @@
         tile = (blk, nv)
         smem = pl.BlockSpec(memory_space=pltpu.SMEM)
         hbm = pl.BlockSpec(memory_space=pltpu.HBM)
-        return pl.pallas_call(
+        vmem = pl.BlockSpec(memory_space=pltpu.VMEM)
+        sums = pl.pallas_call(
             functools.partial(kernel, n_slab, n, ovl, cap),
-            out_shape=pltpu.VMEM(rhs.shape, rhs.dtype),
+            out_shape=[
+                pltpu.VMEM((rows,) + tile, F32),
+                pltpu.VMEM((slots + 1,) + tile, F32),
+                pltpu.SMEM((rows,), jnp.int32),
+            ],
             in_specs=[hbm, hbm, hbm, smem, smem, smem, smem],
-            out_specs=pl.BlockSpec(memory_space=pltpu.VMEM),
+            out_specs=[vmem, vmem, smem],
             scratch_shapes=[
                 pltpu.VMEM(m_blocks.shape[2:], BF16),
                 pltpu.VMEM(j_blocks.shape[2:], BF16),
                 *([pltpu.VMEM((total_rows,) + tile, BF16)] * LENDS),
                 pltpu.VMEM((rows,) + tile, BF16),
-                pltpu.VMEM((rows,) + tile, F32),
-                pltpu.VMEM((slots + 1,) + tile, F32),
                 *([pltpu.VMEM((LENDS, 2, n - 1, cap // 2) + tile, BF16)] * 2),
                 *([pltpu.VMEM((LENDS, 2, 2, ovl // 2) + tile, BF16)] * 2),
                 *([pltpu.VMEM((BACKS, 2, n - 1, cap // 2) + tile, BF16)] * 2),
                 *([pltpu.VMEM((BACKS, 2, 2, ovl // 2) + tile, BF16)] * 2),
                 pltpu.SMEM((slots,), jnp.int32),
-                pltpu.SMEM((rows,), jnp.int32),
                 pltpu.SemaphoreType.DMA((3,)),
                 pltpu.SemaphoreType.DMA((LENDS + BACKS, 2, n + 2)),
                 pltpu.SemaphoreType.DMA((LENDS + BACKS, 2, n + 2)),
@@ -495,6 +507,18 @@
             rhs, m_blocks, j_blocks, m_cols.transpose(0, 3, 1, 2), j_cols.transpose(0, 3, 1, 2),
             send_list.transpose(0, 1, 3, 2), send_count,
         )
+        parts = 4
+        return pl.pallas_call(
+            functools.partial(finish, parts),
+            out_shape=jax.ShapeDtypeStruct(rhs.shape, rhs.dtype),
+            in_specs=[vmem, vmem, smem],
+            out_specs=hbm,
+            scratch_shapes=[
+                pltpu.VMEM((rows,) + tile, BF16),
+                pltpu.SemaphoreType.DMA((parts,)),
+            ],
+            compiler_params=pltpu.CompilerParams(vmem_limit_bytes=16 * 1024 * 1024),
+        )(*[pltpu.with_memory_space_constraint(v, pltpu.VMEM) for v in sums[:2]], sums[2])
 
     return jax.shard_map(
         per_device,

time: 64.8 us -> 64.6 us (level)
  local copies, waits for them, and re-layouts: 0.97 us -> 0 us
  Pallas kernels: 63.6 us -> 64.5 us
    pallas_call x0 -> x1, Pallas kernels: none -> 1.04 us  [per_device(): pl.pallas_call(functools.partial(finish, parts), out_shape=jax.ShapeDtype...]
    unnamed x1 -> x0, local copies, waits for them, and re-layouts: 0.97 us -> none
where the time goes in v5:
time: 64.6 us; the launch traced here: 64.5 us
  Pallas kernels  64.5 us (100%)
    pallas_call x1, Pallas kernels, per_device(): pl.pallas_call(functools.partial(kernel, n_slab, n, ovl, cap), out_shape=...  63.4 us

profile of v5, /device:TPU:0, one launch (start us, length us, event | category | flops | bytes accessed | tf_op | source)
XLA Modules:
  0.0 64.5 jit_solution(1715084859229871230)
XLA Ops:
  0.0 63.4 %shard_map.73 = (f32[32,128,128]{2,1,0:T(8,128)S(1)}, f32[15,128,128]{2,1,0:T(8,128)S(1)}, s32[32]{0:T(128)S(4)}) custom-call(bf16[1,1,32,128,128]{4,3,2,1,0:T(8,128)(2,1)} %rhs_hbm.1, bf16[1,1,56,3,128,128]{5,4,3,2,1,0:T(8,128)(2,1)} %m_hbm.1, bf16[1,1,32,3,128,128]{5,4,3,2,1,0:T(8,128)(2,1)} %j_hbm.1, s32[1,3,1,56]{3,2,1,0:T(1,128)} %bitcast.3, ...), custom_call_target="tpu_custom_call" | custom-call | tf_op jit(solution)/shard_map/pallas_call | solution.py:477
  63.4 1.0 %shard_map.74 = bf16[1,1,32,128,128]{4,3,2,1,0:T(8,128)(2,1)} custom-call(f32[32,128,128]{2,1,0:T(8,128)S(1)} %get-tuple-element.8.acc, f32[15,128,128]{2,1,0:T(8,128)S(1)} %get-tuple-element.9.run, s32[32]{0:T(128)S(4)} %get-tuple-element.10.last), custom_call_target="tpu_custom_call" | custom-call | tf_op jit(solution)/shard_map/pallas_call | solution.py:511
